TPU v7x, 512 devices: a whole 4x8x8 slice. The times are simulated.
512 devices in a mesh: layer: 8 (over z), row: 64 (over y, x, core).
Axes of the slice: x: 4, y: 8, z: 8, core: 2. Of those that a mesh axis runs over, the one named last changes fastest.
Arguments:
- left_factors: bfloat16 [8, 65536, 128], P('layer', 'row'), may hold values from -0.1875 to 0.1875
- right_factors: bfloat16 [8, 65536, 128], P('layer', 'row'), may hold values from -0.1875 to 0.1875
- sketch: bfloat16 [65536, 128], P('row'), may hold values from -0.1875 to 0.1875
- row_basis: bfloat16 [65536, 128], P('row'), may hold values from -0.4375 to 0.4375
- inverse_diag: bfloat16 [65536, 1024], P('row'), may hold values from -0.0625 to 1.44125, as said below
- right_side: bfloat16 [65536, 4096], P('row', 'layer'), may hold values from -6 to 6
- incoming: float32 [128, 4096], P(None, 'layer'), may hold values from -6 to 6
Outputs:
- solution: bfloat16 [65536, 4096], P('row', 'layer')
Inputs may be any that keep to these rules, and one draw needn't show every extreme that they name: `inverse_diag`: each block of 1024 rows is the inverse of that row group's diagonal tile.
All inputs are finite; a program needn't handle non-finite values.
Results may differ from a plain program's by a relative error of at most 0.0095.
Values may be sent and summed in bfloat16 or wider, within the bound.
A program may use at most 128 MiB of HBM per device.

v0:
```python
import jax
import jax.numpy as jnp
from jax import lax
from jax.sharding import PartitionSpec as P


def shifted(value, axis, steps):
    count = lax.axis_size(axis)
    leading, last = (max(0, -steps), min(count, count - steps))
    return lax.ppermute(value, axis, [(source, source + steps) for source in range(leading, last)])


def entering(value, axis, combine, identity):
    count, here = (lax.axis_size(axis), lax.axis_index(axis))
    everything = jax.tree.map(lambda part: lax.all_gather(part, axis), value)
    start = jax.tree.map(
        lambda part, zero: jnp.broadcast_to(jnp.asarray(zero, part.dtype), part.shape),
        value,
        identity,
    )

    def lap(k, before):
        reached = k < here
        new = combine(before, jax.tree.map(lambda part: part[k], everything))
        return jax.tree.map(lambda a, b: jnp.where(reached, a, b), new, before)

    return lax.fori_loop(0, count, lap, start)


def project(basis, vectors):
    return lax.dot_general(
        basis, vectors, (((0,), (0,)), ((), ())), preferred_element_type=jnp.float32
    )


def body(left_factors, right_factors, sketch, row_basis, inverse_diag, right_side, incoming):
    full = lax.Precision.HIGHEST
    rank = sketch.shape[1]
    width = right_side.shape[1]
    core = project(right_factors[0], sketch).astype(jnp.bfloat16)
    partial_range = -jnp.dot(left_factors[0], core, preferred_element_type=jnp.float32)
    tile_range = lax.psum(partial_range, "layer").astype(jnp.bfloat16)
    applied = jnp.dot(inverse_diag, right_side, preferred_element_type=jnp.float32).astype(
        jnp.bfloat16
    )
    gain = jnp.dot(inverse_diag, tile_range, preferred_element_type=jnp.float32).astype(
        jnp.bfloat16
    )

    def combine(earlier, later):
        return (
            jnp.dot(later[0], earlier[0], precision=full),
            jnp.dot(later[0], earlier[1], precision=full) + later[1],
        )

    identity = (jnp.eye(rank, dtype=jnp.float32), jnp.zeros((rank, width), jnp.float32))
    joined = jnp.concatenate([applied, gain], axis=1)
    carried = shifted(joined, "row", 1)
    step_map = -project(row_basis, carried[:, width:])
    step_shift = project(row_basis, carried[:, :width])
    first_group = lax.axis_index("row") == 0
    step_shift = jnp.where(first_group, incoming, step_shift)
    prefix = entering((step_map, step_shift), "row", combine, identity)
    coupled = jnp.dot(step_map, prefix[1], precision=full) + step_shift
    result = applied.astype(jnp.float32) - jnp.dot(
        gain.astype(jnp.float32), coupled, precision=full
    )
    return result.astype(jnp.bfloat16)


def solution(mesh):
    return jax.shard_map(
        body,
        mesh=mesh,
        in_specs=(
            P("layer", "row", None),
            P("layer", "row", None),
            P("row", None),
            P("row", None),
            P("row", None),
            P("row", "layer"),
            P(None, "layer"),
        ),
        out_specs=P("row", "layer"),
        check_vma=False,
    )
```

profile of v0, /device:TPU:1, one launch (start us, length us, event | category | flops | bytes accessed | tf_op | source)
XLA Modules:
  0.0 390.4 jit_solution(16829505180996091301)
XLA Ops:
  6.5 1.8 fusion.8
  8.3 36.2 %all-reduce.1 = bf16[1024,128]{0,1:T(8,128)(2,1)S(1)} all-reduce(f32[1024,128]{0,1:T(8,128)S(1)} %fusion.8), channel_id=1, replica_groups=mesh['layer'=8,'row'=64] {'layer'}, use_global_device_ids=true, to_apply=%region_0.0 | all-reduce | flops 131072 | bytes 786432 | tf_op jit(solution)/shard_map/psum | solution.py:42
  47.2 10.9 %collective-permute-start = (bf16[1024,640]{0,1:T(8,128)(2,1)S(1)}, bf16[1024,640]{0,1:T(8,128)(2,1)S(1)}, u32[]{:S(2)}, u32[]{:S(2)}) collective-permute-start(bf16[1024,640]{0,1:T(8,128)(2,1)S(1)} %pad_maximum_fusion), channel_id=1, source_target_pairs={{0,1},{1,2},{2,3},{3,4},{4,5},{5,6},{6,7},{7,8},{8,9},{9,10},{10,1... | collective-permute-start | bytes 3932168 | tf_op jit(solution)/shard_map/ppermute | solution.py:10
  58.1 14.5 %collective-permute-done = bf16[1024,640]{0,1:T(8,128)(2,1)S(1)} collective-permute-done((bf16[1024,640]{0,1:T(8,128)(2,1)S(1)}, bf16[1024,640]{0,1:T(8,128)(2,1)S(1)}, u32[]{:S(2)}, u32[]{:S(2)}) %collective-permute-start) | collective-permute-done | bytes 1310752 | tf_op jit(solution)/shard_map/ppermute | solution.py:10
  74.7 2.4 fusion.9
  77.1 77.1 %all-gather.5.cloned.1.call-done = f32[8192,128]{0,1:T(8,128)} async-done(((f32[128,128]{0,1:T(8,128)}), f32[8192,128]{0,1:T(8,128)}) %all-gather.5.cloned.1.call-update) | async-done | bytes 4194320 | tf_op jit(solution)/shard_map/all_gather | solution.py:15
  154.2 5.6 %copy.14 = f32[8192,128]{1,0:T(8,128)} copy(f32[8192,128]{0,1:T(8,128)} %all-gather.5.cloned.1.call-done) | data formatting | bytes 8388608
  159.9 108.3 %all-gather.7.cloned.1.call-done = f32[8192,512]{0,1:T(8,128)} async-done(((f32[128,512]{0,1:T(8,128)}), f32[8192,512]{0,1:T(8,128)}) %all-gather.7.cloned.1.call-update) | async-done | bytes 16777232 | tf_op jit(solution)/shard_map/all_gather | solution.py:15
  268.2 17.4 %copy.15 = f32[8192,512]{1,0:T(8,128)} copy(f32[8192,512]{0,1:T(8,128)} %all-gather.7.cloned.1.call-done) | data formatting | bytes 33554432
  285.6 91.2 %while.14 = (s32[]{:T(128)}, f32[128,512]{1,0:T(8,128)S(1)}, s32[]{:T(128)}, f32[64,128,128]{2,1,0:T(8,128)}, f32[64,128,512]{2,1,0:T(8,128)}, /*index=5*/s32[]{:T(128)}, s32[]{:T(128)}) while((s32[]{:T(128)}, f32[128,512]{1,0:T(8,128)S(1)}, s32[]{:T(128)}, f32[64,128,128]{2,1,0:T(8,128)}, f32[64,128,512]{2,1,0:T(8,128)}, ...), condition=%wide.region_2.3_spmd.clone, body=%wide.region_1.2_spmd.clone.sunk | while | flops 100925440 | bytes 1641055 | solution.py:27
  285.6 1.4 fusion.32
  288.5 1.4 fusion.32
  289.9 1.4 fusion.32
  291.3 1.4 fusion.32
  294.2 1.4 fusion.32
  297.0 1.4 fusion.32
  298.5 1.4 fusion.32
  302.7 1.4 fusion.32
  304.1 1.4 fusion.32
  305.6 1.4 fusion.32
  308.4 1.4 fusion.32
  311.3 1.4 fusion.32
  312.7 1.4 fusion.32
  317.0 1.4 fusion.32
  318.4 1.4 fusion.32
  319.8 1.4 fusion.32
  322.7 1.4 fusion.32
  325.5 1.4 fusion.32
  331.2 1.4 fusion.32
  332.6 1.4 fusion.32
  334.1 1.4 fusion.32
  336.9 1.4 fusion.32
  339.8 1.4 fusion.32
  345.5 1.4 fusion.32
  346.9 1.4 fusion.32
  348.3 1.4 fusion.32
  351.2 1.4 fusion.32
  354.0 1.4 fusion.32
  359.7 1.4 fusion.32
  361.1 1.4 fusion.32
  362.6 1.4 fusion.32
  365.4 1.4 fusion.32
  368.3 1.4 fusion.32
  374.0 1.4 fusion.32
  375.4 1.4 fusion.32
  376.8 1.5 convolution_add_fusion.1
  378.3 2.9 subtract_convert_fusion
  381.3 2.3 copy.12
  (117 shorter events, 45.6 us)
Async XLA Ops:
  6.5 38.0 %copy-start = (bf16[1024,1024]{1,0:T(8,128)(2,1)S(1)}, bf16[1024,1024]{1,0:T(8,128)(2,1)}, u32[]{:S(2)}) copy-start(bf16[1024,1024]{1,0:T(8,128)(2,1)} %param.13) | copy-start | bytes 6291460
  6.5 147.7 %all-gather.5.cloned.1.call-start = ((), (), s32[]{:S(2)}) async-start(), calls=%async_computation | async-start | bytes 4259840 | tf_op jit(solution)/shard_map/all_gather | solution.py:15
  44.5 1.2 copy-start.6
  45.8 1.3 copy-start.1
  47.1 25.6 %copy-start.4 = (bf16[1024,128]{1,0:T(8,128)(2,1)S(1)}, bf16[1024,128]{1,0:T(8,128)(2,1)}, u32[]{:S(2)}) copy-start(bf16[1024,128]{1,0:T(8,128)(2,1)} %param.12) | copy-start | bytes 786436
  47.1 26.8 %copy-start.3 = (f32[128,512]{1,0:T(8,128)S(1)}, f32[128,512]{1,0:T(8,128)}, u32[]{:S(2)}) copy-start(f32[128,512]{1,0:T(8,128)} %param.15) | copy-start | bytes 786436
  47.2 25.4 %collective-permute-start = (bf16[1024,640]{0,1:T(8,128)(2,1)S(1)}, bf16[1024,640]{0,1:T(8,128)(2,1)S(1)}, u32[]{:S(2)}, u32[]{:S(2)}) collective-permute-start(bf16[1024,640]{0,1:T(8,128)(2,1)S(1)} %pad_maximum_fusion), channel_id=1, source_target_pairs={{0,1},{1,2},{2,3},{3,4},{4,5},{5,6},{6,7},{7,8},{8,9},{9,10},{10,1... | collective-permute-start | bytes 3932168 | tf_op jit(solution)/shard_map/ppermute | solution.py:10
  72.7 1.1 copy-start.5
  73.8 194.4 %all-gather.7.cloned.1.call-start = ((), (), s32[]{:S(2)}) async-start(), calls=%async_computation.1 | async-start | bytes 17039360 | tf_op jit(solution)/shard_map/all_gather | solution.py:15
  285.6 91.2 %copy-start.2 = (f32[128,128]{1,0:T(8,128)S(1)}, f32[128,128]{1,0:T(8,128)}, u32[]{:S(2)}) copy-start(f32[128,128]{1,0:T(8,128)} %convolution_negate_fusion.1) | copy-start | bytes 196612
Sparse Core Ops, SparseCore 0:
  73.9 80.2 all-gather.4
  157.5 110.6 all-gather.6
where the time goes:
time: 392 us; the launch traced here: 390 us
  waiting for transfers between devices  200 us (51%)
  matrix products  99.5 us (25%)
  blocking collectives  36.2 us (9%)
  local copies, waits for them, and re-layouts  27.8 us (7%)
  between operations  13.5 us (3%)
  starting transfers between devices  10.9 us (3%)
    all_gather x2, waiting for transfers between devices, entering(): everything = jax.tree.map(lambda part: lax.all_gather(part, axis), value)  185 us
    dot_general x64, matrix products, combine(): jnp.dot(later[0], earlier[1], precision=full) + later[1]  87.6 us
    psum x1, blocking collectives, body(): tile_range = lax.psum(partial_range, 'layer').astype(jnp.bfloat16)  36.2 us
    unnamed x17, local copies, waits for them, and re-layouts  24.3 us
    ppermute x1, waiting for transfers between devices, shifted(): lax.ppermute(value, axis, [(source, source + steps) for source in range(l...  14.5 us
    ppermute x1, starting transfers between devices, shifted(): lax.ppermute(value, axis, [(source, source + steps) for source in range(l...  10.9 us
  transfers between devices with their start and end apart: 3, of which 3 were waited for; matrix products, arithmetic and copies ran while one was open for 2% of the time, Pallas kernels for 0%

commit v1 on v0

--- a/solution.py
+++ b/solution.py
@@ -2,6 +2,12 @@
 import jax.numpy as jnp
 from jax import lax
 from jax.sharding import PartitionSpec as P
+
+
+def add_all(value, mesh_axis):
+    parts = lax.all_gather(value, mesh_axis, axis=0, tiled=False)
+    acc = parts.sum(axis=0)
+    return acc
 
 
 def shifted(value, axis, steps):
@@ -39,7 +45,7 @@
     width = right_side.shape[1]
     core = project(right_factors[0], sketch).astype(jnp.bfloat16)
     partial_range = -jnp.dot(left_factors[0], core, preferred_element_type=jnp.float32)
-    tile_range = lax.psum(partial_range, "layer").astype(jnp.bfloat16)
+    tile_range = add_all(partial_range, "layer").astype(jnp.bfloat16)
     applied = jnp.dot(inverse_diag, right_side, preferred_element_type=jnp.float32).astype(
         jnp.bfloat16
     )

time: 392 us -> 420 us (1.071)
  waiting for transfers between devices: 200 us -> 262 us
  blocking collectives: 36.2 us -> 0 us
  starting transfers between devices: 10.9 us -> 3.91 us
  local copies, waits for them, and re-layouts: 27.8 us -> 33.6 us
    all_gather x0 -> x1, waiting for transfers between devices: none -> 61.2 us  [add_all(): parts = lax.all_gather(value, mesh_axis, axis=0, tiled=False)]
    psum x1 -> x0, blocking collectives: 36.2 us -> none  [body(): tile_range = lax.psum(partial_range, 'layer').astype(jnp.bfloat16)]
    ppermute x1, starting transfers between devices: 10.9 us -> 3.83 us  [shifted(): lax.ppermute(value, axis, [(source, source + steps) for source in range(l...]
    unnamed x17 -> x16, local copies, waits for them, and re-layouts: 24.3 us -> 30.1 us
  transfers between devices with their start and end apart: 3 -> 4, of which waited for: 3 -> 4; matrix products, arithmetic and copies ran while one was open for 2% -> 3% of each run, Pallas kernels for 0% -> 0%
where the time goes in v1:
time: 420 us; the launch traced here: 418 us
  waiting for transfers between devices  262 us (62%)
  matrix products  101 us (24%)
  local copies, waits for them, and re-layouts  33.6 us (8%)
  between operations  13.2 us (3%)
    all_gather x2, waiting for transfers between devices, entering(): everything = jax.tree.map(lambda part: lax.all_gather(part, axis), value)  186 us
    dot_general x64, matrix products, combine(): jnp.dot(later[0], earlier[1], precision=full) + later[1]  87.6 us
    all_gather x1, waiting for transfers between devices, add_all(): parts = lax.all_gather(value, mesh_axis, axis=0, tiled=False)  61.2 us
    unnamed x16, local copies, waits for them, and re-layouts  30.1 us
    ppermute x1, waiting for transfers between devices, shifted(): lax.ppermute(value, axis, [(source, source + steps) for source in range(l...  14.5 us
  transfers between devices with their start and end apart: 4, of which 4 were waited for; matrix products, arithmetic and copies ran while one was open for 3% of the time, Pallas kernels for 0%

profile of v1, /device:TPU:1, one launch (start us, length us, event | category | flops | bytes accessed | tf_op | source)
XLA Modules:
  0.0 417.9 jit_solution(14221680552633576290)
XLA Ops:
  6.5 2.6 fusion.8
  9.2 2.5 convolution_convert_fusion
  11.7 61.2 %all-gather.7.cloned.1.call-done = f32[8192,128]{0,1:T(8,128)} async-done(((f32[1024,128]{0,1:T(8,128)}), f32[8192,128]{0,1:T(8,128)}) %all-gather.7.cloned.1.call-update) | async-done | bytes 4194320 | tf_op jit(solution)/shard_map/all_gather | solution.py:8
  73.0 5.4 %copy.21 = f32[16,8,8,1024]{3,2,1,0:T(8,128)S(1)} copy(f32[16,8,8,1024]{3,1,2,0:T(8,128)} %bitcast.44) | data formatting | bytes 8388608
  81.1 3.8 collective-permute-start
  84.9 14.5 %collective-permute-done = bf16[1024,640]{0,1:T(8,128)(2,1)S(1)} collective-permute-done((bf16[1024,640]{0,1:T(8,128)(2,1)S(1)}, bf16[1024,640]{0,1:T(8,128)(2,1)S(1)}, u32[]{:S(2)}, u32[]{:S(2)}) %collective-permute-start) | collective-permute-done | bytes 1310752 | tf_op jit(solution)/shard_map/ppermute | solution.py:16
  101.5 2.4 fusion.9
  103.9 78.2 %all-gather.9.cloned.1.call-done = f32[8192,128]{0,1:T(8,128)} async-done(((f32[128,128]{0,1:T(8,128)}), f32[8192,128]{0,1:T(8,128)}) %all-gather.9.cloned.1.call-update) | async-done | bytes 4194320 | tf_op jit(solution)/shard_map/all_gather | solution.py:21
  182.1 5.6 %copy.19 = f32[8192,128]{1,0:T(8,128)} copy(f32[8192,128]{0,1:T(8,128)} %all-gather.9.cloned.1.call-done) | data formatting | bytes 8388608
  187.7 108.3 %all-gather.11.cloned.1.call-done = f32[8192,512]{0,1:T(8,128)} async-done(((f32[128,512]{0,1:T(8,128)}), f32[8192,512]{0,1:T(8,128)}) %all-gather.11.cloned.1.call-update) | async-done | bytes 16777232 | tf_op jit(solution)/shard_map/all_gather | solution.py:21
  296.0 17.4 %copy.20 = f32[8192,512]{1,0:T(8,128)} copy(f32[8192,512]{0,1:T(8,128)} %all-gather.11.cloned.1.call-done) | data formatting | bytes 33554432
  313.5 91.2 %while.14 = (s32[]{:T(128)}, f32[128,512]{1,0:T(8,128)S(1)}, s32[]{:T(128)}, f32[64,128,128]{2,1,0:T(8,128)}, f32[64,128,512]{2,1,0:T(8,128)}, /*index=5*/s32[]{:T(128)}, s32[]{:T(128)}) while((s32[]{:T(128)}, f32[128,512]{1,0:T(8,128)S(1)}, s32[]{:T(128)}, f32[64,128,128]{2,1,0:T(8,128)}, f32[64,128,512]{2,1,0:T(8,128)}, ...), condition=%wide.region_2.3_spmd.clone, body=%wide.region_1.2_spmd.clone.sunk | while | flops 100925440 | bytes 1641055 | solution.py:33
  313.5 1.4 fusion.32
  316.3 1.4 fusion.32
  317.8 1.4 fusion.32
  322.0 1.4 fusion.32
  323.4 1.4 fusion.32
  324.9 1.4 fusion.32
  327.7 1.4 fusion.32
  330.6 1.4 fusion.32
  336.3 1.4 fusion.32
  337.7 1.4 fusion.32
  339.1 1.4 fusion.32
  342.0 1.4 fusion.32
  344.8 1.4 fusion.32
  350.5 1.4 fusion.32
  351.9 1.4 fusion.32
  353.4 1.4 fusion.32
  356.2 1.4 fusion.32
  359.1 1.4 fusion.32
  364.8 1.4 fusion.32
  366.2 1.4 fusion.32
  367.6 1.4 fusion.32
  370.5 1.4 fusion.32
  373.3 1.4 fusion.32
  379.0 1.4 fusion.32
  380.4 1.4 fusion.32
  381.9 1.4 fusion.32
  384.7 1.4 fusion.32
  387.6 1.4 fusion.32
  393.3 1.4 fusion.32
  394.7 1.4 fusion.32
  396.1 1.4 fusion.32
  399.0 1.4 fusion.32
  401.8 1.4 fusion.32
  404.6 1.5 convolution_add_fusion.1
  406.2 2.9 subtract_convert_fusion
  409.1 2.3 copy.17
  (119 shorter events, 48.4 us)
Async XLA Ops:
  6.5 2.6 copy-start
  6.5 66.4 %all-gather.7.cloned.1.call-start = ((), (), s32[]{:S(2)}) async-start(), calls=%async_computation | async-start | bytes 4718592 | tf_op jit(solution)/shard_map/all_gather | solution.py:8
  9.1 173.0 %all-gather.9.cloned.1.call-start = ((), (), s32[]{:S(2)}) async-start(), calls=%async_computation.1 | async-start | bytes 4259840 | tf_op jit(solution)/shard_map/all_gather | solution.py:21
  79.4 20.0 %copy-start.4 = (bf16[1024,128]{1,0:T(8,128)(2,1)S(1)}, bf16[1024,128]{1,0:T(8,128)(2,1)}, u32[]{:S(2)}) copy-start(bf16[1024,128]{1,0:T(8,128)(2,1)} %param.12) | copy-start | bytes 786436
  80.3 0.7 copy-start.1
  80.3 20.3 %copy-start.3 = (f32[128,512]{1,0:T(8,128)S(1)}, f32[128,512]{1,0:T(8,128)}, u32[]{:S(2)}) copy-start(f32[128,512]{1,0:T(8,128)} %param.15) | copy-start | bytes 786436
  81.1 18.4 %collective-permute-start = (bf16[1024,640]{0,1:T(8,128)(2,1)S(1)}, bf16[1024,640]{0,1:T(8,128)(2,1)S(1)}, u32[]{:S(2)}, u32[]{:S(2)}) collective-permute-start(bf16[1024,640]{0,1:T(8,128)(2,1)S(1)} %pad_maximum_fusion), channel_id=1, source_target_pairs={{0,1},{1,2},{2,3},{3,4},{4,5},{5,6},{6,7},{7,8},{8,9},{9,10},{10,1... | collective-permute-start | bytes 3932168 | tf_op jit(solution)/shard_map/ppermute | solution.py:16
  99.4 1.1 copy-start.5
  100.6 195.4 %all-gather.11.cloned.1.call-start = ((), (), s32[]{:S(2)}) async-start(), calls=%async_computation.2 | async-start | bytes 17039360 | tf_op jit(solution)/shard_map/all_gather | solution.py:21
  313.5 91.2 %copy-start.2 = (f32[128,128]{1,0:T(8,128)S(1)}, f32[128,128]{1,0:T(8,128)}, u32[]{:S(2)}) copy-start(f32[128,128]{1,0:T(8,128)} %convolution_negate_fusion.1) | copy-start | bytes 196612
Sparse Core Ops, SparseCore 0:
  9.4 63.4 all-gather.6
  100.7 81.3 all-gather.8
  185.3 110.6 all-gather.10
